TPU v7x, 32 devices: a whole 2x2x4 slice. The times are simulated.
32 devices in a mesh: dp: 8 (over y, x, core), tensor: 4 (over z).
Axes of the slice: x: 2, y: 2, z: 4, core: 2. Of those that a mesh axis runs over, the one named last changes fastest.
Arguments:
- tokens: bfloat16 [8192, 1536], P('dp'), may hold values from -6 to 6
- block_order: int32 [1, 8], replicated, may hold values from 0 to 7, each once within a row
- attn_gain: float32 [1536], replicated, may hold values from 0.5 to 1.5
- w_query: bfloat16 [1536, 1536], P(None, 'tensor'), may hold values from -0.15625 to 0.15625
- w_key: bfloat16 [1536, 768], P(None, 'tensor'), may hold values from -0.15625 to 0.15625
- w_value: bfloat16 [1536, 768], P(None, 'tensor'), may hold values from -0.15625 to 0.15625
- w_out: bfloat16 [1536, 1536], P('tensor'), may hold values from -1.25 to 1.25
- mlp_gain: float32 [1536], replicated, may hold values from 0.5 to 1.5
- w_gate: bfloat16 [1536, 4096], P(None, 'tensor'), may hold values from -0.15625 to 0.15625
- w_up: bfloat16 [1536, 4096], P(None, 'tensor'), may hold values from -0.15625 to 0.15625
- w_down: bfloat16 [4096, 1536], P('tensor'), may hold values from -0.09375 to 0.09375
- cotangent: bfloat16 [8192, 1536], P('dp'), may hold values from -6 to 6
Outputs:
- activations: bfloat16 [8192, 1536], P('dp')
- grad_tokens: bfloat16 [8192, 1536], P('dp')
- grad_attn_gain: float32 [1536], replicated
- grad_query: float32 [1536, 1536], P(None, 'tensor')
- grad_key: float32 [1536, 768], P(None, 'tensor')
- grad_value: float32 [1536, 768], P(None, 'tensor')
- grad_out: float32 [1536, 1536], P('tensor')
- grad_mlp_gain: float32 [1536], replicated
- grad_gate: float32 [1536, 4096], P(None, 'tensor')
- grad_up: float32 [1536, 4096], P(None, 'tensor')
- grad_down: float32 [4096, 1536], P('tensor')
Inputs may be any that keep to these rules, and one draw needn't show every extreme that they name: `block_order`: entry j of row g is the prompt block of 512 tokens held by the j-th device of group g; each row is a permutation.
All inputs are finite; a program needn't handle non-finite values.
Results may differ from a plain program's by a relative error of at most 0.02.
Values may be sent and summed in bfloat16 or wider, within the bound.
A program may use at most 192 MiB of HBM per device.

v0:
```python
import jax
import jax.numpy as jnp
from jax import lax
from jax.sharding import PartitionSpec as P

HEAD_DIM = 96
GROUP_DEVS = 8
PB = 512
CL = 512
EPSILON = 1e-05
ROTARY_BASE = 100000.0


def from_partner(value, axis, distance):
    mask = 2**distance
    pairs = [(source, source ^ mask) for source in range(lax.axis_size(axis))]
    return lax.ppermute(value, axis, pairs)


def rotary_tables(places):
    halfway = HEAD_DIM // 2
    frequency = ROTARY_BASE ** (-(jnp.arange(halfway, dtype=jnp.float32) * 2.0) / HEAD_DIM)
    angle = places.astype(jnp.float32)[:, None] * frequency[None, :]
    cosine_table = jnp.concatenate([jnp.cos(angle), jnp.cos(angle)], axis=-1)
    sine_table = jnp.concatenate([jnp.sin(angle), jnp.sin(angle)], axis=-1)
    return (cosine_table, sine_table)


def rotate(inputs, cosine_table, sine_table):
    halfway = inputs.shape[-1] // 2
    shaped = (inputs.shape[0],) + (1,) * (inputs.ndim - 2) + (inputs.shape[-1],)
    turned = jnp.concatenate([-inputs[..., halfway:], inputs[..., :halfway]], axis=-1)
    return inputs * cosine_table.reshape(shaped) + turned * sine_table.reshape(shaped)


def product(former, latter):
    return jnp.dot(former, latter, preferred_element_type=jnp.float32)


def weight_grad(former, latter):
    return lax.dot_general(
        former, latter, (((0,), (0,)), ((), ())), preferred_element_type=jnp.float32
    )


def input_grad(former, latter):
    return lax.dot_general(
        former, latter, (((1,), (1,)), ((), ())), preferred_element_type=jnp.float32
    )


def rms_inverse(inputs):
    return lax.rsqrt(jnp.mean(inputs * inputs, axis=-1, keepdims=True) + EPSILON)


def norm_back(inputs, inverse, gain, upstream):
    inner = upstream * gain
    through = inverse * inner - inputs * inverse**3 * jnp.mean(
        inner * inputs, axis=-1, keepdims=True
    )
    return (through, jnp.sum(upstream * inputs * inverse, axis=0))


def shards(
    tokens,
    block_order,
    attn_gain,
    w_query,
    w_key,
    w_value,
    w_out,
    mlp_gain,
    w_gate,
    w_up,
    w_down,
    cotangent,
):
    device = lax.axis_index("dp")
    member = device % GROUP_DEVS
    group_index = device // GROUP_DEVS
    order_row = lax.dynamic_index_in_dim(block_order, group_index, 0, keepdims=False)
    own_block = lax.dynamic_index_in_dim(order_row, member, 0, keepdims=False)
    offsets = jnp.arange(PB, dtype=jnp.int32)
    prompt_places = order_row[:, None] * PB + offsets[None, :]
    tail_places = GROUP_DEVS * PB + jnp.arange(CL, dtype=jnp.int32)
    places = jnp.concatenate([own_block * PB + offsets, tail_places])
    cosine_table, sine_table = rotary_tables(places)
    token_count = tokens.shape[0]
    key_heads = w_key.shape[1] // HEAD_DIM
    repeat = w_query.shape[1] // HEAD_DIM // key_heads
    factor = HEAD_DIM ** (-0.5)
    inputs = tokens.astype(jnp.float32)
    inverse_one = rms_inverse(inputs)
    normed = (inputs * inverse_one * attn_gain).astype(jnp.bfloat16)
    queries = rotate(
        product(normed, w_query).reshape(token_count, key_heads, repeat, HEAD_DIM),
        cosine_table,
        sine_table,
    ).astype(jnp.bfloat16)
    key_set = rotate(
        product(normed, w_key).reshape(token_count, key_heads, HEAD_DIM), cosine_table, sine_table
    ).astype(jnp.bfloat16)
    value_set = (
        product(normed, w_value).reshape(token_count, key_heads, HEAD_DIM).astype(jnp.bfloat16)
    )
    levels = GROUP_DEVS.bit_length() - 1
    stacked = jnp.stack([key_set[:PB], value_set[:PB]])[:, None]
    for level in range(levels):
        partner = from_partner(stacked, "dp", level)
        upper = member // 2**level % 2 == 1
        stacked = jnp.where(
            upper,
            jnp.concatenate([partner, stacked], axis=1),
            jnp.concatenate([stacked, partner], axis=1),
        )
    prompt_keys = stacked[0]
    prompt_values = stacked[1]
    tail_keys = key_set[PB:]
    tail_values = value_set[PB:]

    def scores(key_block, key_places):
        products = (
            jnp.einsum("qkrd,nkd->krqn", queries, key_block, preferred_element_type=jnp.float32)
            * factor
        )
        visible = key_places[None, None, None, :] <= places[None, None, :, None]
        return (products, visible)

    def total_step(running, block):
        summit, totals = running
        products, visible = scores(block[0], block[1])
        masked = jnp.where(visible, products, -1e30)
        higher = jnp.maximum(summit, jnp.max(masked, axis=-1))
        totals = totals * jnp.exp(summit - higher) + jnp.sum(
            jnp.where(visible, jnp.exp(masked - higher[..., None]), 0.0), axis=-1
        )
        return ((higher, totals), None)

    start = (
        jnp.full((key_heads, repeat, token_count), -1e30, jnp.float32),
        jnp.zeros((key_heads, repeat, token_count), jnp.float32),
    )
    running, _ = lax.scan(total_step, start, (prompt_keys, prompt_places))
    running, _ = total_step(running, (tail_keys, tail_places))
    log_total = running[0] + jnp.log(running[1])

    def chances_of(products, visible):
        return jnp.where(visible, jnp.exp(products - log_total[..., None]), 0.0)

    def output_step(summed, block):
        products, visible = scores(block[0], block[2])
        weights = chances_of(products, visible).astype(jnp.bfloat16)
        return (
            summed
            + jnp.einsum("krqn,nkd->qkrd", weights, block[1], preferred_element_type=jnp.float32),
            None,
        )

    empty_heads = jnp.zeros((token_count, key_heads, repeat, HEAD_DIM), jnp.float32)
    attended, _ = lax.scan(output_step, empty_heads, (prompt_keys, prompt_values, prompt_places))
    attended, _ = output_step(attended, (tail_keys, tail_values, tail_places))
    attended_low = attended.reshape(token_count, -1).astype(jnp.bfloat16)
    attention = lax.psum(product(attended_low, w_out).astype(jnp.bfloat16), "tensor").astype(
        jnp.float32
    )
    middle = inputs + attention
    inverse_two = rms_inverse(middle)
    normed_two = (middle * inverse_two * mlp_gain).astype(jnp.bfloat16)
    gate_pre = product(normed_two, w_gate)
    up_pre = product(normed_two, w_up)
    sigmoid_gate = jax.nn.sigmoid(gate_pre)
    hidden = (gate_pre * sigmoid_gate * up_pre).astype(jnp.bfloat16)
    feed_out = lax.psum(product(hidden, w_down).astype(jnp.bfloat16), "tensor").astype(jnp.float32)
    activations = (middle + feed_out).astype(jnp.bfloat16)
    upstream = cotangent.astype(jnp.float32)
    grad_hidden = input_grad(cotangent, w_down)
    grad_gate_low = (
        grad_hidden * up_pre * sigmoid_gate * (1.0 + gate_pre * (1.0 - sigmoid_gate))
    ).astype(jnp.bfloat16)
    grad_up_low = (grad_hidden * gate_pre * sigmoid_gate).astype(jnp.bfloat16)
    grad_w_gate = weight_grad(normed_two, grad_gate_low)
    grad_w_up = weight_grad(normed_two, grad_up_low)
    grad_w_down = weight_grad(hidden, cotangent)
    grad_normed_two = lax.psum(
        (input_grad(grad_gate_low, w_gate) + input_grad(grad_up_low, w_up)).astype(jnp.bfloat16),
        "tensor",
    ).astype(jnp.float32)
    through_two, grad_gain_two = norm_back(middle, inverse_two, mlp_gain, grad_normed_two)
    grad_middle = upstream + through_two
    grad_attention = grad_middle.astype(jnp.bfloat16)
    grad_w_out = weight_grad(attended_low, grad_attention)
    grad_attended = (
        input_grad(grad_attention, w_out)
        .reshape(token_count, key_heads, repeat, HEAD_DIM)
        .astype(jnp.bfloat16)
    )
    row_inner = jnp.transpose(
        jnp.sum(grad_attended.astype(jnp.float32) * attended, axis=-1), (1, 2, 0)
    )

    def back_step(grad_queries, block):
        products, visible = scores(block[0], block[2])
        chances = chances_of(products, visible)
        grad_chances = jnp.einsum(
            "qkrd,nkd->krqn", grad_attended, block[1], preferred_element_type=jnp.float32
        )
        grad_scores = (chances * (grad_chances - row_inner[..., None])).astype(jnp.bfloat16)
        grad_queries = (
            grad_queries
            + jnp.einsum(
                "krqn,nkd->qkrd", grad_scores, block[0], preferred_element_type=jnp.float32
            )
            * factor
        )
        grad_keys = (
            jnp.einsum("krqn,qkrd->nkd", grad_scores, queries, preferred_element_type=jnp.float32)
            * factor
        )
        grad_values = jnp.einsum(
            "krqn,qkrd->nkd",
            chances.astype(jnp.bfloat16),
            grad_attended,
            preferred_element_type=jnp.float32,
        )
        return (grad_queries, (grad_keys, grad_values))

    grad_queries, prompt_grads = lax.scan(
        back_step, empty_heads, (prompt_keys, prompt_values, prompt_places)
    )
    grad_queries, tail_grads = back_step(grad_queries, (tail_keys, tail_values, tail_places))
    pending = jnp.stack([prompt_grads[0], prompt_grads[1]])
    for level in reversed(range(levels)):
        halfway = pending.shape[1] // 2
        upper = member // 2**level % 2 == 1
        kept_part = jnp.where(upper, pending[:, halfway:], pending[:, :halfway])
        sent_part = jnp.where(upper, pending[:, :halfway], pending[:, halfway:])
        pending = kept_part + from_partner(sent_part.astype(jnp.bfloat16), "dp", level).astype(
            sent_part.dtype
        )
    grad_key_rot = jnp.concatenate([pending[0, 0], tail_grads[0]])
    grad_value_all = jnp.concatenate([pending[1, 0], tail_grads[1]])
    grad_query_low = (
        rotate(grad_queries, cosine_table, -sine_table)
        .reshape(token_count, -1)
        .astype(jnp.bfloat16)
    )
    grad_key_low = (
        rotate(grad_key_rot, cosine_table, -sine_table)
        .reshape(token_count, -1)
        .astype(jnp.bfloat16)
    )
    grad_value_low = grad_value_all.reshape(token_count, -1).astype(jnp.bfloat16)
    grad_w_query = weight_grad(normed, grad_query_low)
    grad_w_key = weight_grad(normed, grad_key_low)
    grad_w_value = weight_grad(normed, grad_value_low)
    grad_normed = lax.psum(
        (
            input_grad(grad_query_low, w_query)
            + input_grad(grad_key_low, w_key)
            + input_grad(grad_value_low, w_value)
        ).astype(jnp.bfloat16),
        "tensor",
    ).astype(jnp.float32)
    through_one, grad_gain_one = norm_back(inputs, inverse_one, attn_gain, grad_normed)
    grad_tokens = (grad_middle + through_one).astype(jnp.bfloat16)
    shares = (
        lax.psum_scatter(grad_gain_one, "dp", scatter_dimension=0, tiled=True),
        lax.psum_scatter(grad_w_query, "dp", scatter_dimension=0, tiled=True),
        lax.psum_scatter(grad_w_key, "dp", scatter_dimension=0, tiled=True),
        lax.psum_scatter(grad_w_value, "dp", scatter_dimension=0, tiled=True),
        lax.psum_scatter(grad_w_out, "dp", scatter_dimension=1, tiled=True),
        lax.psum_scatter(grad_gain_two, "dp", scatter_dimension=0, tiled=True),
        lax.psum_scatter(grad_w_gate, "dp", scatter_dimension=0, tiled=True),
        lax.psum_scatter(grad_w_up, "dp", scatter_dimension=0, tiled=True),
        lax.psum_scatter(grad_w_down, "dp", scatter_dimension=1, tiled=True),
    )
    summed_grads = (
        lax.all_gather(shares[0].astype(jnp.bfloat16), "dp", axis=0, tiled=True).astype(
            jnp.float32
        ),
        lax.all_gather(shares[1].astype(jnp.bfloat16), "dp", axis=0, tiled=True).astype(
            jnp.float32
        ),
        lax.all_gather(shares[2].astype(jnp.bfloat16), "dp", axis=0, tiled=True).astype(
            jnp.float32
        ),
        lax.all_gather(shares[3].astype(jnp.bfloat16), "dp", axis=0, tiled=True).astype(
            jnp.float32
        ),
        lax.all_gather(shares[4].astype(jnp.bfloat16), "dp", axis=1, tiled=True).astype(
            jnp.float32
        ),
        lax.all_gather(shares[5].astype(jnp.bfloat16), "dp", axis=0, tiled=True).astype(
            jnp.float32
        ),
        lax.all_gather(shares[6].astype(jnp.bfloat16), "dp", axis=0, tiled=True).astype(
            jnp.float32
        ),
        lax.all_gather(shares[7].astype(jnp.bfloat16), "dp", axis=0, tiled=True).astype(
            jnp.float32
        ),
        lax.all_gather(shares[8].astype(jnp.bfloat16), "dp", axis=1, tiled=True).astype(
            jnp.float32
        ),
    )
    return (activations, grad_tokens) + tuple(summed_grads)


def solution(mesh):
    in_specs = (
        P("dp", None),
        P(),
        P(),
        P(None, "tensor"),
        P(None, "tensor"),
        P(None, "tensor"),
        P("tensor", None),
        P(),
        P(None, "tensor"),
        P(None, "tensor"),
        P("tensor", None),
        P("dp", None),
    )
    out_specs = (
        P("dp", None),
        P("dp", None),
        P(),
        P(None, "tensor"),
        P(None, "tensor"),
        P(None, "tensor"),
        P("tensor", None),
        P(),
        P(None, "tensor"),
        P(None, "tensor"),
        P("tensor", None),
    )
    return jax.shard_map(shards, mesh=mesh, in_specs=in_specs, out_specs=out_specs, check_vma=False)
```

profile of v0, /device:TPU:0, one launch (start us, length us, event | category | flops | bytes accessed | tf_op | source)
XLA Modules:
  0.0 1503.1 jit_solution(2448952385256326114)
XLA Ops:
  32.2 14.5 collective-permute-done.1
  62.4 6.5 fusion.59
  68.9 17.4 %collective-permute-done.2 = bf16[2,4,512,2,96]{2,4,3,0,1:T(8,128)(2,1)} collective-permute-done((bf16[2,4,512,2,96]{2,4,3,0,1:T(8,128)(2,1)}, bf16[2,4,512,2,96]{2,4,3,0,1:T(8,128)(2,1)}, u32[]{:S(2)}, u32[]{:S(2)}) %collective-permute-start.2) | collective-permute-done | bytes 1572896 | tf_op jit(solution)/shard_map/ppermute | solution.py:17
  91.4 92.3 %while.39 = (s32[]{:T(128)}, f32[2,2,1024]{2,1,0:T(2,128)S(1)}, f32[2,2,1024]{2,1,0:T(2,128)S(1)}, s32[8,512]{1,0:T(8,128)S(1)}, s32[1024]{0:T(1024)S(1)}, /*ind...) while((s32[]{:T(128)}, f32[2,2,1024]{2,1,0:T(2,128)S(1)}, ...), condition=%wide.region_4.5_spmd.clone, body=%wide.region_1.4_spmd.clone.sunk | while | flops 419975168 | bytes 21654152 | solution.py:143
  91.8 6.4 fusion.203
  103.4 6.4 fusion.203
  114.9 6.4 fusion.203
  126.4 6.4 fusion.203
  138.0 6.4 fusion.203
  149.5 6.4 fusion.203
  161.0 6.4 fusion.203
  172.6 6.4 fusion.203
  189.0 74.2 %while.40 = (s32[]{:T(128)}, f32[1024,2,2,96]{0,3,2,1:T(8,128)}, bf16[8,512,2,96]{1,3,2,0:T(8,128)(2,1)}, s32[8,512]{1,0:T(8,128)S(1)}, s32[1024]{0:T(1024)S(1)}...) while((s32[]{:T(128)}, f32[1024,2,2,96]{0,3,2,1:T(8,128)}, ...), condition=%wide.region_8.9_spmd.clone, body=%wide.region_7.8_spmd.clone.sunk | while | flops 815005696 | bytes 6646447 | solution.py:160
  200.8 6.3 bitcast_add_fusion.6
  210.1 6.3 bitcast_add_fusion.6
  219.4 6.3 bitcast_add_fusion.6
  228.7 6.3 bitcast_add_fusion.6
  238.1 6.3 bitcast_add_fusion.6
  247.4 6.3 bitcast_add_fusion.6
  256.7 6.3 bitcast_add_fusion.6
  263.2 7.2 fusion.99
  274.8 122.4 %all-reduce.11.cloned.1.call-done = bf16[1024,1536]{1,0:T(8,128)(2,1)} async-done(((bf16[1024,1536]{1,0:T(8,128)(2,1)}), bf16[1024,1536]{1,0:T(8,128)(2,1)}) %all-reduce.11.cloned.1.call-update) | async-done | bytes 3145744 | tf_op jit(solution)/shard_map/psum | solution.py:163
  412.4 8.3 multiply_convert_fusion.1
  431.5 120.2 %all-reduce.13.cloned.1.call-done = bf16[1024,1536]{1,0:T(8,128)(2,1)} async-done(((bf16[1024,1536]{1,0:T(8,128)(2,1)}), bf16[1024,1536]{1,0:T(8,128)(2,1)}) %all-reduce.13.cloned.1.call-update) | async-done | bytes 3145744 | tf_op jit(solution)/shard_map/psum | solution.py:184
  551.7 7.0 fusion.71
  571.7 181.7 %while.41 = (s32[]{:T(128)}, f32[1024,2,2,96]{0,3,2,1:T(8,128)}, f32[8,512,2,96]{1,3,2,0:T(8,128)}, f32[8,512,2,96]{1,3,2,0:T(8,128)}, bf16[8,512,2,96]{1,3,2,0:...) while((s32[]{:T(128)}, f32[1024,2,2,96]{0,3,2,1:T(8,128)}, ...), condition=%wide.region_16.17_spmd.clone, body=%wide.region_15.16_spmd.clone.sunk | while | flops 2036039680 | bytes 111014752 | solution.py:227
  588.4 6.4 fusion.223
  634.1 6.0 fusion.223
  767.3 8.7 fusion.124
  776.1 9.0 fusion.125
  785.1 8.7 fusion.126
  799.0 37.8 %collective-permute-done.3 = bf16[2,4,512,2,96]{2,4,3,1,0:T(8,128)(2,1)S(1)} collective-permute-done((bf16[2,4,512,2,96]{2,4,3,1,0:T(8,128)(2,1)S(1)}, bf16[2,4,512,2,96]{2,4,3,1,0:T(8,128)(2,1)S(1)}, u32[]{:S(2)}, u32[]{:S(2)}) %collective-permute-start.3) | collective-permute-done | bytes 1572896 | tf_op jit(solution)/shard_map/ppermute | solution.py:17
  842.3 33.1 %collective-permute-done.4 = bf16[2,2,512,2,96]{2,4,3,1,0:T(8,128)(2,1)S(1)} collective-permute-done((bf16[2,2,512,2,96]{2,4,3,1,0:T(8,128)(2,1)S(1)}, bf16[2,2,512,2,96]{2,4,3,1,0:T(8,128)(2,1)S(1)}, u32[]{:S(2)}, u32[]{:S(2)}) %collective-permute-start.4) | collective-permute-done | bytes 786464 | tf_op jit(solution)/shard_map/ppermute | solution.py:17
  894.9 6.5 convolution_convert_fusion.1
  909.5 50.2 %reduce-scatter.18.cloned.1.call-done = f32[192,1024]{1,0:T(8,128)} async-done(((f32[1536,1024]{1,0:T(8,128)}), f32[192,1024]{1,0:T(8,128)}) %reduce-scatter.18.cloned.1.call-update) | async-done | bytes 786448 | tf_op jit(solution)/shard_map/reduce_scatter | solution.py:274
  961.7 63.1 %reduce-scatter.20.cloned.1.call-done = f32[1024,192]{0,1:T(8,128)} async-done(((f32[1024,1536]{0,1:T(8,128)}), f32[1024,192]{0,1:T(8,128)}) %reduce-scatter.20.cloned.1.call-update) | async-done | bytes 786448 | tf_op jit(solution)/shard_map/reduce_scatter | solution.py:275
  1028.7 38.3 %reduce-scatter.12.cloned.1.call-done = f32[192,192]{1,0:T(8,128)} async-done(((f32[1536,192]{1,0:T(8,128)}), f32[192,192]{1,0:T(8,128)}) %reduce-scatter.12.cloned.1.call-update) | async-done | bytes 147472 | tf_op jit(solution)/shard_map/reduce_scatter | solution.py:270
  1067.9 11.3 all_gather.30
  1081.7 27.5 %reduce-scatter.10.cloned.1.call-done = f32[192,192]{1,0:T(8,128)} async-done(((f32[1536,192]{1,0:T(8,128)}), f32[192,192]{1,0:T(8,128)}) %reduce-scatter.10.cloned.1.call-update) | async-done | bytes 147472 | tf_op jit(solution)/shard_map/reduce_scatter | solution.py:269
  1110.1 11.3 all_gather.29
  1123.8 11.3 all-gather.8.cloned.1.call-done
  1137.8 24.0 %all-gather.6.cloned.1.call-done = bf16[1536,384]{1,0:T(8,128)(2,1)} async-done(((bf16[192,384]{1,0:T(8,128)(2,1)}), bf16[1536,384]{1,0:T(8,128)(2,1)}) %all-gather.6.cloned.1.call-update) | async-done | bytes 1179664 | tf_op jit(solution)/shard_map/all_gather | solution.py:281
  1164.6 223.4 %all-reduce.15.cloned.1.call-done = (bf16[1024,1536]{1,0:T(8,128)(2,1)}, bf16[1024,1536]{1,0:T(8,128)(2,1)}) async-done(((bf16[1024,1536]{1,0:T(8,128)(2,1)}, bf16[1024,1536]{1,0:T(8,128)(2,1)}), (bf16[1024,1536]{1,0:T(8,128)(2,1)}, bf16[1024,1536]{1,0:T(8,128)(2,1)})) %all-reduce.15.cloned.1.call-update) | async-done | bytes 6291472 | tf_op jit(solution)/shard_map/psum | solution.py:173
  1392.5 24.4 %all-reduce.4 = (bf16[1536]{0:T(1024)(128)(2,1)S(1)}, bf16[1536]{0:T(1024)(128)(2,1)S(1)}) all-reduce(f32[1536]{0:T(1024)S(1)} %get-tuple-element.291, f32[1536]{0:T(1024)S(1)} %copy-done.62), channel_id=2, replica_groups=mesh['dp'=8,'tensor'=4] {'dp'}, use_global_device_ids=true, to_apply=%region_20.21.clone | all-reduce | flops 3072 | bytes 18432
  1417.5 12.4 all-reduce.5
  1431.1 10.3 fusion.66
  1446.8 9.6 all-gather.12.cloned.1.call-done
  1461.8 28.9 %all-gather.14.cloned.1.call-done = bf16[1024,1536]{0,1:T(8,128)(2,1)} async-done(((bf16[1024,192]{0,1:T(8,128)(2,1)}), bf16[1024,1536]{0,1:T(8,128)(2,1)}) %all-gather.14.cloned.1.call-update) | async-done | bytes 3145744 | tf_op jit(solution)/shard_map/all_gather | solution.py:302
  (566 shorter events, 423.0 us)
Async XLA Ops:
  7.2 405.2 %copy-start = (bf16[1024,1536]{1,0:T(8,128)(2,1)S(1)}, bf16[1024,1536]{1,0:T(8,128)(2,1)}, u32[]{:S(2)}) copy-start(bf16[1024,1536]{1,0:T(8,128)(2,1)} %param.28) | copy-start | bytes 9437188
  7.2 8.0 copy-start.57
  7.2 390.0 %all-reduce.11.cloned.1.call-start = ((), (), s32[]{:S(2)}) async-start(), calls=%async_computation.7 | async-start | bytes 6291456 | tf_op jit(solution)/shard_map/psum | solution.py:163
  7.3 7.9 copy-start.5
  11.7 41.5 %copy-start.16 = (f32[1024,96]{0,1:T(8,128)}, f32[1024,96]{0,1:T(8,128)S(1)}, u32[]{:S(2)}) copy-start(f32[1024,96]{0,1:T(8,128)S(1)} %pad_maximum_fusion.2) | copy-start | bytes 1179652
  21.1 2.1 collective-permute-start
  25.7 21.0 %collective-permute-start.1 = (bf16[2,2,512,2,96]{2,4,3,0,1:T(8,128)(2,1)}, bf16[2,2,512,2,96]{2,4,3,0,1:T(8,128)(2,1)}, u32[]{:S(2)}, u32[]{:S(2)}) collective-permute-start(bf16[2,2,512,2,96]{2,4,3,0,1:T(8,128)(2,1)} %maximum_select_fusion.2), channel_id=1, source_target_pairs={{0,8},{4,12},{8,0},{12,4},{16,24},{20,28},{24,16},{28,20},{1,9},{5... | collective-permute-start | bytes 2359304 | tf_op jit(solution)/shard_map/ppermute | solution.py:17
  32.2 19.7 %copy-start.18 = (f32[1024,384]{0,1:T(8,128)}, f32[1024,384]{0,1:T(8,128)S(1)}, u32[]{:S(2)}) copy-start(f32[1024,384]{0,1:T(8,128)S(1)} %fusion.116) | copy-start | bytes 4718596
  50.1 36.2 %collective-permute-start.2 = (bf16[2,4,512,2,96]{2,4,3,0,1:T(8,128)(2,1)}, bf16[2,4,512,2,96]{2,4,3,0,1:T(8,128)(2,1)}, u32[]{:S(2)}, u32[]{:S(2)}) collective-permute-start(bf16[2,4,512,2,96]{2,4,3,0,1:T(8,128)(2,1)} %maximum_select_fusion.1), channel_id=1, source_target_pairs={{0,16},{4,20},{8,24},{12,28},{16,0},{20,4},{24,8},{28,12},{1,17},{... | collective-permute-start | bytes 4718600 | tf_op jit(solution)/shard_map/ppermute | solution.py:17
  189.0 74.2 %copy-start.54 = (bf16[512,192]{0,1:T(8,128)(2,1)S(1)}, bf16[512,192]{0,1:T(8,128)(2,1)}, u32[]{:S(2)}) copy-start(bf16[512,192]{0,1:T(8,128)(2,1)} %get-tuple-element.370) | copy-start | bytes 589828
  263.2 8.1 copy-start.70
  274.8 126.5 %copy-start.59 = (f32[1536]{0:T(1024)S(1)}, f32[1536]{0:T(1024)}, u32[]{:S(2)}) copy-start(f32[1536]{0:T(1024)} %param.25) | copy-start | bytes 18436
  274.8 276.9 %all-reduce.13.cloned.1.call-start = ((), (), s32[]{:S(2)}) async-start(), calls=%async_computation.8 | async-start | bytes 6291456 | tf_op jit(solution)/shard_map/psum | solution.py:184
  431.4 459.7 %reduce-scatter.14.cloned.1.call-start = ((), (), s32[]{:S(2)}) async-start(), calls=%async_computation.13 | async-start | bytes 2654208 | tf_op jit(solution)/shard_map/reduce_scatter | solution.py:271
  551.7 7.0 copy-start.7
  551.7 7.0 copy-start.9
  551.7 7.0 copy-start.15
  569.1 323.8 %reduce-scatter.8.cloned.1.call-start = ((), (), s32[]{:S(2)}) async-start(), calls=%async_computation.9 | async-start | bytes 2654208 | tf_op jit(solution)/shard_map/reduce_scatter | solution.py:268
  575.2 6.6 copy-start.2
  620.5 6.5 copy-start.2
  643.1 6.5 copy-start.2
  665.8 6.5 copy-start.2
  688.5 6.5 copy-start.2
  711.2 6.5 copy-start.2
  733.8 6.5 copy-start.2
  767.0 140.3 %reduce-scatter.16.cloned.1.call-start = ((), (), s32[]{:S(2)}) async-start(), calls=%async_computation.15 | async-start | bytes 7077888 | tf_op jit(solution)/shard_map/reduce_scatter | solution.py:273
  776.0 183.7 %reduce-scatter.18.cloned.1.call-start = ((), (), s32[]{:S(2)}) async-start(), calls=%async_computation.17 | async-start | bytes 7077888 | tf_op jit(solution)/shard_map/reduce_scatter | solution.py:274
  785.1 239.7 %reduce-scatter.20.cloned.1.call-start = ((), (), s32[]{:S(2)}) async-start(), calls=%async_computation.19 | async-start | bytes 7077888 | tf_op jit(solution)/shard_map/reduce_scatter | solution.py:275
  793.8 273.1 %reduce-scatter.12.cloned.1.call-start = ((), (), s32[]{:S(2)}) async-start(), calls=%async_computation.12 | async-start | bytes 1769472 | tf_op jit(solution)/shard_map/reduce_scatter | solution.py:270
  794.1 81.9 %slice-start = ((s8[8388608]{0:T(1024)(128)(4,1)}), s8[4194304]{0:T(1024)(128)(4,1)S(1)}, s32[]{:S(2)}) async-start(s8[8388608]{0:T(1024)(128)(4,1)} %bitcast.300), calls=%async_computation.22 | async-start | bytes 8388608
  797.6 78.4 %slice-start.1 = ((s8[8388608]{0:T(1024)(128)(4,1)}), s8[4194304]{0:T(1024)(128)(4,1)S(1)}, s32[]{:S(2)}) async-start(s8[8388608]{0:T(1024)(128)(4,1)} %bitcast.300), calls=%async_computation.23 | async-start | bytes 8388608
  797.6 39.2 %collective-permute-start.3 = (bf16[2,4,512,2,96]{2,4,3,1,0:T(8,128)(2,1)S(1)}, bf16[2,4,512,2,96]{2,4,3,1,0:T(8,128)(2,1)S(1)}, u32[]{:S(2)}, u32[]{:S(2)}) collective-permute-start(bf16[2,4,512,2,96]{2,4,3,1,0:T(8,128)(2,1)S(1)} %select_convert_fusion), channel_id=1, source_target_pairs={{0,16},{4,20},{8,24},{12,28},{16,0},{20,4},{24,8},{28,12},{1,17},{... | collective-permute-start | bytes 4718600 | tf_op jit(solution)/shard_map/ppermute | solution.py:17
  840.8 35.2 %copy-start.35 = (pred[1024,512]{0,1:T(8,128)(4,1)S(1)}, pred[1024,512]{0,1:T(8,128)(4,1)}, u32[]{:S(2)}) copy-start(pred[1024,512]{0,1:T(8,128)(4,1)} %copy-done.34) | copy-start | bytes 1572868
  840.8 35.2 %copy-start.46 = (bf16[1024,2,2,96]{0,3,2,1:T(8,128)(2,1)S(1)}, bf16[1024,2,2,96]{0,3,2,1:T(8,128)(2,1)}, u32[]{:S(2)}) copy-start(bf16[1024,2,2,96]{0,3,2,1:T(8,128)(2,1)} %get-tuple-element.726) | copy-start | bytes 2359300
  840.8 35.2 %copy-start.66 = (f32[2,2,1024]{2,1,0:T(2,128)S(1)}, f32[2,2,1024]{2,1,0:T(2,128)}, u32[]{:S(2)}) copy-start(f32[2,2,1024]{2,1,0:T(2,128)} %get-tuple-element.741) | copy-start | bytes 49156
  840.8 34.5 %collective-permute-start.4 = (bf16[2,2,512,2,96]{2,4,3,1,0:T(8,128)(2,1)S(1)}, bf16[2,2,512,2,96]{2,4,3,1,0:T(8,128)(2,1)S(1)}, u32[]{:S(2)}, u32[]{:S(2)}) collective-permute-start(bf16[2,2,512,2,96]{2,4,3,1,0:T(8,128)(2,1)S(1)} %select_convert_fusion.1), channel_id=1, source_target_pairs={{0,8},{4,12},{8,0},{12,4},{16,24},{20,28},{24,16},{28,20},{1,9},{5... | collective-permute-start | bytes 2359304 | tf_op jit(solution)/shard_map/ppermute | solution.py:17
  875.9 2.1 collective-permute-start.5
  882.6 226.5 %reduce-scatter.10.cloned.1.call-start = ((), (), s32[]{:S(2)}) async-start(), calls=%async_computation.11 | async-start | bytes 1769472 | tf_op jit(solution)/shard_map/reduce_scatter | solution.py:269
  891.1 244.0 %all-gather.8.cloned.1.call-start = ((), (), s32[]{:S(2)}) async-start(), calls=%async_computation.14 | async-start | bytes 1327104 | tf_op jit(solution)/shard_map/all_gather | solution.py:290
  892.8 269.0 %all-gather.6.cloned.1.call-start = ((), (), s32[]{:S(2)}) async-start(), calls=%async_computation.10 | async-start | bytes 1327104 | tf_op jit(solution)/shard_map/all_gather | solution.py:281
  894.6 493.4 %all-reduce.15.cloned.1.call-start = ((), (), s32[]{:S(2)}) async-start(), calls=%async_computation.21 | async-start | bytes 12582912 | tf_op jit(solution)/shard_map/psum | solution.py:173
  907.3 119.5 %copy-start.67 = (u32[32]{0:T(128)S(1)}, u32[32]{0:T(128)}, u32[]{:S(2)}) copy-start(u32[32]{0:T(128)} %constant.181) | copy-start | bytes 388
  907.3 534.1 %all-gather.10.cloned.1.call-start = ((), (), s32[]{:S(2)}) async-start(), calls=%async_computation.16 | async-start | bytes 3538944 | tf_op jit(solution)/shard_map/all_gather | solution.py:296
  909.4 547.0 %all-gather.12.cloned.1.call-start = ((), (), s32[]{:S(2)}) async-start(), calls=%async_computation.18 | async-start | bytes 3538944 | tf_op jit(solution)/shard_map/all_gather | solution.py:299
  961.6 529.0 %all-gather.14.cloned.1.call-start = ((), (), s32[]{:S(2)}) async-start(), calls=%async_computation.20 | async-start | bytes 3538944 | tf_op jit(solution)/shard_map/all_gather | solution.py:302
  1123.8 264.2 %copy-start.58 = (f32[1536]{0:T(1024)S(1)}, f32[1536]{0:T(1024)}, u32[]{:S(2)}) copy-start(f32[1536]{0:T(1024)} %param.20) | copy-start | bytes 18436
  1123.8 264.2 %copy-start.61 = (f32[1024]{0:T(1024)S(1)}, f32[1024]{0:T(1024)}, u32[]{:S(2)}) copy-start(f32[1024]{0:T(1024)} %copy-done.60) | copy-start | bytes 12292
  1388.0 43.1 %copy-start.64 = (f32[1024]{0:T(1024)S(1)}, f32[1024]{0:T(1024)}, u32[]{:S(2)}) copy-start(f32[1024]{0:T(1024)} %get-tuple-element.376) | copy-start | bytes 12292
  (118 other events, 437.5 us)
Sparse Core Ops, SparseCore 0:
  274.9 122.2 all-reduce.10
  431.6 120.0 all-reduce.12
  569.2 41.5 reduce-scatter.13
  767.2 44.7 reduce-scatter.7
  815.8 77.8 reduce-scatter.15
  897.9 61.7 reduce-scatter.17
  963.1 61.7 reduce-scatter.19
  1028.5 38.4 reduce-scatter.11
  1070.6 38.4 reduce-scatter.9
  1111.0 24.0 all-gather.7
  1137.7 24.0 all-gather.5
  1164.8 223.1 all-reduce.14
  1390.6 31.4 all-gather.9
  1424.0 32.3 all-gather.11
  1458.3 32.3 all-gather.13
where the time goes:
time: 1510 us; the launch traced here: 1500 us
  waiting for transfers between devices  824 us (55%)
  matrix products  379 us (25%)
  other arithmetic  151 us (10%)
  local copies, waits for them, and re-layouts  62.3 us (4%)
  blocking collectives  59.4 us (4%)
  between operations  16.7 us (1%)
    psum x1, waiting for transfers between devices, shards(): lax.psum(product(hidden, w_down).astype(jnp.bfloat16), 'tensor')  223 us
    psum x1, waiting for transfers between devices, shards(): lax.psum(product(attended_low, w_out).astype(jnp.bfloat16), 'tensor')  122 us
    psum x1, waiting for transfers between devices, shards(): lax.psum((input_grad(grad_gate_low, w_gate) + input_grad(grad_up_low, w_u...  120 us
    ppermute x6, waiting for transfers between devices, from_partner(): return lax.ppermute(value, axis, pairs)  104 us
    dot_general x17, matrix products, scores(): jnp.einsum('qkrd,nkd->krqn', queries, key_block, preferred_element_type=j...  78.6 us
    reduce_scatter x1, waiting for transfers between devices, shards(): lax.psum_scatter(grad_w_down, 'dp', scatter_dimension=1, tiled=True)  63.1 us
    dot_general x9, matrix products, output_step(): jnp.einsum('krqn,nkd->qkrd', weights, block[1], preferred_element_type=jn...  57.3 us
    dot_general x9, matrix products, back_step(): jnp.einsum('krqn,qkrd->nkd', chances.astype(jnp.bfloat16), grad_attended,...  50.4 us
  transfers between devices with their start and end apart: 21, of which 16 were waited for; matrix products, arithmetic and copies ran while one was open for 20% of the time, Pallas kernels for 0%

commit v1 on v0

--- a/solution.py
+++ b/solution.py
@@ -9,6 +9,10 @@
 CL = 512
 EPSILON = 1e-05
 ROTARY_BASE = 100000.0
+
+
+def trace_table_here(inp):
+    return lax.all_gather(inp, axis_name="tensor").sum(axis=0)
 
 
 def from_partner(value, axis, distance):
@@ -181,9 +185,8 @@
     grad_w_gate = weight_grad(normed_two, grad_gate_low)
     grad_w_up = weight_grad(normed_two, grad_up_low)
     grad_w_down = weight_grad(hidden, cotangent)
-    grad_normed_two = lax.psum(
-        (input_grad(grad_gate_low, w_gate) + input_grad(grad_up_low, w_up)).astype(jnp.bfloat16),
-        "tensor",
+    grad_normed_two = trace_table_here(
+        (input_grad(grad_gate_low, w_gate) + input_grad(grad_up_low, w_up)).astype(jnp.bfloat16)
     ).astype(jnp.float32)
     through_two, grad_gain_two = norm_back(middle, inverse_two, mlp_gain, grad_normed_two)
     grad_middle = upstream + through_two

time: 1510 us -> 1490 us (0.987)
  waiting for transfers between devices: 824 us -> 772 us
  local copies, waits for them, and re-layouts: 62.3 us -> 85.7 us
    all_gather x0 -> x1, waiting for transfers between devices: none -> 189 us  [trace_table_here(): return lax.all_gather(inp, axis_name='tensor').sum(axis=0)]
    psum x1 -> x0, waiting for transfers between devices: 120 us -> none  [shards(): lax.psum((input_grad(grad_gate_low, w_gate) + input_grad(grad_up_low, w_u...]
    reduce_scatter x1, waiting for transfers between devices: 63.1 us -> 0.02 us  [shards(): lax.psum_scatter(grad_w_down, 'dp', scatter_dimension=1, tiled=True)]
    reduce_scatter x1, waiting for transfers between devices: 50.2 us -> 0.02 us  [shards(): lax.psum_scatter(grad_w_up, 'dp', scatter_dimension=0, tiled=True)]
    dynamic_slice x40, local copies, waits for them, and re-layouts: 14.7 us -> 32.3 us  [shards(): running, _ = lax.scan(total_step, start, (prompt_keys, prompt_places))]
    unnamed x142 -> x148, local copies, waits for them, and re-layouts: 28.6 us -> 33.7 us
  transfers between devices with their start and end apart: 21 -> 21, of which waited for: 16 -> 14; matrix products, arithmetic and copies ran while one was open for 20% -> 22% of each run, Pallas kernels for 0% -> 0%
where the time goes in v1:
time: 1490 us; the launch traced here: 1480 us
  waiting for transfers between devices  772 us (52%)
  matrix products  382 us (26%)
  other arithmetic  158 us (11%)
  local copies, waits for them, and re-layouts  85.7 us (6%)
  blocking collectives  58.8 us (4%)
  between operations  16.7 us (1%)
    psum x1, waiting for transfers between devices, shards(): lax.psum(product(hidden, w_down).astype(jnp.bfloat16), 'tensor')  223 us
    all_gather x1, waiting for transfers between devices, trace_table_here(): return lax.all_gather(inp, axis_name='tensor').sum(axis=0)  189 us
    psum x1, waiting for transfers between devices, shards(): lax.psum(product(attended_low, w_out).astype(jnp.bfloat16), 'tensor')  122 us
    ppermute x6, waiting for transfers between devices, from_partner(): return lax.ppermute(value, axis, pairs)  93.5 us
    dot_general x17, matrix products, scores(): jnp.einsum('qkrd,nkd->krqn', queries, key_block, preferred_element_type=j...  79.4 us
    dot_general x9, matrix products, output_step(): jnp.einsum('krqn,nkd->qkrd', weights, block[1], preferred_element_type=jn...  57.3 us
    dot_general x9, matrix products, back_step(): jnp.einsum('krqn,qkrd->nkd', chances.astype(jnp.bfloat16), grad_attended,...  51.7 us
    dot_general x9, matrix products, back_step(): jnp.einsum('qkrd,nkd->krqn', grad_attended, block[1], preferred_element_t...  41.8 us
  transfers between devices with their start and end apart: 21, of which 14 were waited for; matrix products, arithmetic and copies ran while one was open for 22% of the time, Pallas kernels for 0%

profile of v1, /device:TPU:0, one launch (start us, length us, event | category | flops | bytes accessed | tf_op | source)
XLA Modules:
  0.0 1484.9 jit_solution(10507020753001668974)
XLA Ops:
  32.2 14.5 collective-permute-done.1
  62.8 6.4 fusion.59
  69.2 17.0 %collective-permute-done.2 = bf16[2,4,512,2,96]{2,4,3,0,1:T(8,128)(2,1)} collective-permute-done((bf16[2,4,512,2,96]{2,4,3,0,1:T(8,128)(2,1)}, bf16[2,4,512,2,96]{2,4,3,0,1:T(8,128)(2,1)}, u32[]{:S(2)}, u32[]{:S(2)}) %collective-permute-start.2) | collective-permute-done | bytes 1572896 | tf_op jit(solution)/shard_map/ppermute | solution.py:21
  91.1 98.7 %while.39 = (s32[]{:T(128)}, f32[2,2,1024]{2,1,0:T(2,128)S(1)}, f32[2,2,1024]{2,1,0:T(2,128)S(1)}, s32[8,512]{1,0:T(8,128)}, s32[1024]{0:T(1024)S(1)}, /*index=5...) while((s32[]{:T(128)}, f32[2,2,1024]{2,1,0:T(2,128)S(1)}, ...), condition=%wide.region_4.5_spmd.clone, body=%wide.region_1.4_spmd.clone.sunk | while | flops 419975168 | bytes 21654152 | solution.py:147
  92.2 6.5 fusion.203
  104.6 6.5 fusion.203
  116.9 6.5 fusion.203
  129.3 6.5 fusion.203
  141.6 6.5 fusion.203
  153.9 6.5 fusion.203
  166.3 6.5 fusion.203
  178.6 6.5 fusion.203
  195.1 79.9 %while.40 = (s32[]{:T(128)}, f32[1024,2,2,96]{0,3,2,1:T(8,128)}, bf16[8,512,2,96]{1,3,2,0:T(8,128)(2,1)}, s32[8,512]{1,0:T(8,128)}, s32[1024]{0:T(1024)S(1)}, /*...) while((s32[]{:T(128)}, f32[1024,2,2,96]{0,3,2,1:T(8,128)}, ...), condition=%wide.region_8.9_spmd.clone, body=%wide.region_7.8_spmd.clone.sunk | while | flops 815005696 | bytes 6515319 | solution.py:164
  208.4 6.3 bitcast_add_fusion.6
  218.4 6.3 bitcast_add_fusion.6
  228.4 6.3 bitcast_add_fusion.6
  238.4 6.3 bitcast_add_fusion.6
  248.5 6.3 bitcast_add_fusion.6
  258.5 6.3 bitcast_add_fusion.6
  268.5 6.3 bitcast_add_fusion.6
  275.0 7.2 fusion.99
  286.7 122.4 %all-reduce.10.cloned.1.call-done = bf16[1024,1536]{1,0:T(8,128)(2,1)} async-done(((bf16[1024,1536]{1,0:T(8,128)(2,1)}), bf16[1024,1536]{1,0:T(8,128)(2,1)}) %all-reduce.10.cloned.1.call-update) | async-done | bytes 3145744 | tf_op jit(solution)/shard_map/psum | solution.py:167
  424.2 8.3 multiply_convert_fusion.1
  443.3 9.3 fusion.124
  452.9 9.2 fusion.125
  462.1 8.7 fusion.126
  471.4 189.2 %all-gather.18.cloned.1.call-done = bf16[4096,1536]{1,0:T(8,128)(2,1)} async-done(((bf16[1024,1536]{1,0:T(8,128)(2,1)}), bf16[4096,1536]{1,0:T(8,128)(2,1)}) %all-gather.18.cloned.1.call-update) | async-done | bytes 12582928 | tf_op jit(solution)/shard_map/all_gather | solution.py:15
  660.6 9.1 reduce_sum.96
  669.8 7.3 fusion.71
  691.3 191.1 %while.41 = (s32[]{:T(128)}, f32[1024,2,2,96]{0,3,2,1:T(8,128)}, f32[8,512,2,96]{1,3,2,0:T(8,128)}, f32[8,512,2,96]{1,3,2,0:T(8,128)}, bf16[8,512,2,96]{1,3,2,0:...) while((s32[]{:T(128)}, f32[1024,2,2,96]{0,3,2,1:T(8,128)}, ...), condition=%wide.region_16.17_spmd.clone, body=%wide.region_15.16_spmd.clone.sunk | while | flops 2036039680 | bytes 111014752 | solution.py:230
  731.7 6.5 fusion.223
  804.3 7.1 fusion.223
  829.0 6.2 fusion.223
  907.5 41.2 %collective-permute-done.3 = bf16[2,4,512,2,96]{2,4,3,1,0:T(8,128)(2,1)S(1)} collective-permute-done((bf16[2,4,512,2,96]{2,4,3,1,0:T(8,128)(2,1)S(1)}, bf16[2,4,512,2,96]{2,4,3,1,0:T(8,128)(2,1)S(1)}, u32[]{:S(2)}, u32[]{:S(2)}) %collective-permute-start.3) | collective-permute-done | bytes 1572896 | tf_op jit(solution)/shard_map/ppermute | solution.py:21
  954.3 19.1 %collective-permute-done.4 = bf16[2,2,512,2,96]{2,4,3,1,0:T(8,128)(2,1)S(1)} collective-permute-done((bf16[2,2,512,2,96]{2,4,3,1,0:T(8,128)(2,1)S(1)}, bf16[2,2,512,2,96]{2,4,3,1,0:T(8,128)(2,1)S(1)}, u32[]{:S(2)}, u32[]{:S(2)}) %collective-permute-start.4) | collective-permute-done | bytes 786464 | tf_op jit(solution)/shard_map/ppermute | solution.py:21
  993.0 6.5 convolution_convert_fusion.1
  1013.3 15.0 %all-gather.14.cloned.1.call-done = bf16[1536,1024]{1,0:T(8,128)(2,1)} async-done(((bf16[192,1024]{1,0:T(8,128)(2,1)}), bf16[1536,1024]{1,0:T(8,128)(2,1)}) %all-gather.14.cloned.1.call-update) | async-done | bytes 3145744 | tf_op jit(solution)/shard_map/all_gather | solution.py:302
  1033.6 28.9 %all-gather.16.cloned.1.call-done = bf16[1024,1536]{0,1:T(8,128)(2,1)} async-done(((bf16[1024,192]{0,1:T(8,128)(2,1)}), bf16[1024,1536]{0,1:T(8,128)(2,1)}) %all-gather.16.cloned.1.call-update) | async-done | bytes 3145744 | tf_op jit(solution)/shard_map/all_gather | solution.py:305
  1067.9 36.8 %reduce-scatter.12.cloned.1.call-done = f32[192,192]{1,0:T(8,128)} async-done(((f32[1536,192]{1,0:T(8,128)}), f32[192,192]{1,0:T(8,128)}) %reduce-scatter.12.cloned.1.call-update) | async-done | bytes 147472 | tf_op jit(solution)/shard_map/reduce_scatter | solution.py:273
  1105.6 11.3 all_gather.38
  1119.4 27.3 %reduce-scatter.10.cloned.1.call-done = f32[192,192]{1,0:T(8,128)} async-done(((f32[1536,192]{1,0:T(8,128)}), f32[192,192]{1,0:T(8,128)}) %reduce-scatter.10.cloned.1.call-update) | async-done | bytes 147472 | tf_op jit(solution)/shard_map/reduce_scatter | solution.py:272
  1147.6 11.3 all_gather.37
  1161.3 11.5 all-gather.10.cloned.1.call-done
  1175.5 23.9 %all-gather.8.cloned.1.call-done = bf16[1536,384]{1,0:T(8,128)(2,1)} async-done(((bf16[192,384]{1,0:T(8,128)(2,1)}), bf16[1536,384]{1,0:T(8,128)(2,1)}) %all-gather.8.cloned.1.call-update) | async-done | bytes 1179664 | tf_op jit(solution)/shard_map/all_gather | solution.py:284
  1202.2 223.4 %all-reduce.12.cloned.1.call-done = (bf16[1024,1536]{1,0:T(8,128)(2,1)}, bf16[1024,1536]{1,0:T(8,128)(2,1)}) async-done(((bf16[1024,1536]{1,0:T(8,128)(2,1)}, bf16[1024,1536]{1,0:T(8,128)(2,1)}), (bf16[1024,1536]{1,0:T(8,128)(2,1)}, bf16[1024,1536]{1,0:T(8,128)(2,1)})) %all-reduce.12.cloned.1.call-update) | async-done | bytes 6291472 | tf_op jit(solution)/shard_map/psum | solution.py:177
  1430.1 24.0 %all-reduce.4 = (bf16[1536]{0:T(1024)(128)(2,1)S(1)}, bf16[1536]{0:T(1024)(128)(2,1)S(1)}) all-reduce(f32[1536]{0:T(1024)S(1)} %get-tuple-element.291, f32[1536]{0:T(1024)S(1)} %copy-done.64), channel_id=3, replica_groups=mesh['dp'=8,'tensor'=4] {'dp'}, use_global_device_ids=true, to_apply=%region_20.21.clone | all-reduce | flops 3072 | bytes 18432
  1454.7 12.1 all-reduce.5
  1468.0 9.9 fusion.66
  (541 shorter events, 440.0 us)
Async XLA Ops:
  7.2 417.0 %copy-start = (bf16[1024,1536]{1,0:T(8,128)(2,1)S(1)}, bf16[1024,1536]{1,0:T(8,128)(2,1)}, u32[]{:S(2)}) copy-start(bf16[1024,1536]{1,0:T(8,128)(2,1)} %param.28) | copy-start | bytes 9437188
  7.2 7.9 copy-start.59
  7.2 401.8 %all-reduce.10.cloned.1.call-start = ((), (), s32[]{:S(2)}) async-start(), calls=%async_computation.7 | async-start | bytes 6291456 | tf_op jit(solution)/shard_map/psum | solution.py:167
  7.3 7.8 copy-start.5
  11.7 41.3 %copy-start.16 = (f32[1024,96]{0,1:T(8,128)}, f32[1024,96]{0,1:T(8,128)S(1)}, u32[]{:S(2)}) copy-start(f32[1024,96]{0,1:T(8,128)S(1)} %pad_maximum_fusion.2) | copy-start | bytes 1179652
  21.1 2.1 collective-permute-start
  25.7 21.0 %collective-permute-start.1 = (bf16[2,2,512,2,96]{2,4,3,0,1:T(8,128)(2,1)}, bf16[2,2,512,2,96]{2,4,3,0,1:T(8,128)(2,1)}, u32[]{:S(2)}, u32[]{:S(2)}) collective-permute-start(bf16[2,2,512,2,96]{2,4,3,0,1:T(8,128)(2,1)} %maximum_select_fusion.2), channel_id=1, source_target_pairs={{0,8},{4,12},{8,0},{12,4},{16,24},{20,28},{24,16},{28,20},{1,9},{5... | collective-permute-start | bytes 2359304 | tf_op jit(solution)/shard_map/ppermute | solution.py:21
  32.2 19.5 %copy-start.18 = (f32[1024,384]{0,1:T(8,128)}, f32[1024,384]{0,1:T(8,128)S(1)}, u32[]{:S(2)}) copy-start(f32[1024,384]{0,1:T(8,128)S(1)} %fusion.116) | copy-start | bytes 4718596
  49.9 36.2 %collective-permute-start.2 = (bf16[2,4,512,2,96]{2,4,3,0,1:T(8,128)(2,1)}, bf16[2,4,512,2,96]{2,4,3,0,1:T(8,128)(2,1)}, u32[]{:S(2)}, u32[]{:S(2)}) collective-permute-start(bf16[2,4,512,2,96]{2,4,3,0,1:T(8,128)(2,1)} %maximum_select_fusion.1), channel_id=1, source_target_pairs={{0,16},{4,20},{8,24},{12,28},{16,0},{20,4},{24,8},{28,12},{1,17},{... | collective-permute-start | bytes 4718600 | tf_op jit(solution)/shard_map/ppermute | solution.py:21
  195.1 79.9 %copy-start.57 = (bf16[512,192]{0,1:T(8,128)(2,1)S(1)}, bf16[512,192]{0,1:T(8,128)(2,1)}, u32[]{:S(2)}) copy-start(bf16[512,192]{0,1:T(8,128)(2,1)} %get-tuple-element.370) | copy-start | bytes 589828
  275.0 8.1 copy-start.71
  286.6 126.5 %copy-start.61 = (f32[1536]{0:T(1024)S(1)}, f32[1536]{0:T(1024)}, u32[]{:S(2)}) copy-start(f32[1536]{0:T(1024)} %param.25) | copy-start | bytes 18436
  286.6 374.0 %all-gather.18.cloned.1.call-start = ((), (), s32[]{:S(2)}) async-start(), calls=%async_computation.20 | async-start | bytes 15728640 | tf_op jit(solution)/shard_map/all_gather | solution.py:15
  443.3 452.8 %reduce-scatter.16.cloned.1.call-start = ((), (), s32[]{:S(2)}) async-start(), calls=%async_computation.14 | async-start | bytes 7077888 | tf_op jit(solution)/shard_map/reduce_scatter | solution.py:276
  452.6 445.5 %reduce-scatter.18.cloned.1.call-start = ((), (), s32[]{:S(2)}) async-start(), calls=%async_computation.16 | async-start | bytes 7077888 | tf_op jit(solution)/shard_map/reduce_scatter | solution.py:277
  462.1 438.0 %reduce-scatter.20.cloned.1.call-start = ((), (), s32[]{:S(2)}) async-start(), calls=%async_computation.18 | async-start | bytes 7077888 | tf_op jit(solution)/shard_map/reduce_scatter | solution.py:278
  470.9 518.4 %reduce-scatter.14.cloned.1.call-start = ((), (), s32[]{:S(2)}) async-start(), calls=%async_computation.12 | async-start | bytes 2654208 | tf_op jit(solution)/shard_map/reduce_scatter | solution.py:274
  669.7 7.3 copy-start.7
  669.7 7.9 copy-start.9
  669.7 9.0 copy-start.12
  691.0 300.0 %reduce-scatter.8.cloned.1.call-start = ((), (), s32[]{:S(2)}) async-start(), calls=%async_computation.8 | async-start | bytes 2654208 | tf_op jit(solution)/shard_map/reduce_scatter | solution.py:271
  691.2 191.1 %copy-start.58 = (bf16[512,192]{0,1:T(8,128)(2,1)S(1)}, bf16[512,192]{0,1:T(8,128)(2,1)}, u32[]{:S(2)}) copy-start(bf16[512,192]{0,1:T(8,128)(2,1)} %get-tuple-element.370) | copy-start | bytes 589828
  695.1 6.6 copy-start.2
  718.0 6.6 copy-start.2
  742.2 6.7 copy-start.2
  766.7 6.6 copy-start.2
  790.2 6.6 copy-start.2
  815.2 6.6 copy-start.2
  838.9 6.6 copy-start.2
  862.5 6.6 copy-start.2
  895.9 112.0 %all-gather.12.cloned.1.call-start = ((), (), s32[]{:S(2)}) async-start(), calls=%async_computation.15 | async-start | bytes 3538944 | tf_op jit(solution)/shard_map/all_gather | solution.py:299
  898.0 130.3 %all-gather.14.cloned.1.call-start = ((), (), s32[]{:S(2)}) async-start(), calls=%async_computation.17 | async-start | bytes 3538944 | tf_op jit(solution)/shard_map/all_gather | solution.py:302
  900.0 162.5 %all-gather.16.cloned.1.call-start = ((), (), s32[]{:S(2)}) async-start(), calls=%async_computation.19 | async-start | bytes 3538944 | tf_op jit(solution)/shard_map/all_gather | solution.py:305
  902.1 202.6 %reduce-scatter.12.cloned.1.call-start = ((), (), s32[]{:S(2)}) async-start(), calls=%async_computation.11 | async-start | bytes 1769472 | tf_op jit(solution)/shard_map/reduce_scatter | solution.py:273
  902.3 71.7 %slice-start = ((s8[8388608]{0:T(1024)(128)(4,1)}), s8[4194304]{0:T(1024)(128)(4,1)S(1)}, s32[]{:S(2)}) async-start(s8[8388608]{0:T(1024)(128)(4,1)} %bitcast.302), calls=%async_computation.22 | async-start | bytes 8388608
  905.7 68.3 %slice-start.1 = ((s8[8388608]{0:T(1024)(128)(4,1)}), s8[4194304]{0:T(1024)(128)(4,1)S(1)}, s32[]{:S(2)}) async-start(s8[8388608]{0:T(1024)(128)(4,1)} %bitcast.302), calls=%async_computation.23 | async-start | bytes 8388608
  905.8 42.9 %collective-permute-start.3 = (bf16[2,4,512,2,96]{2,4,3,1,0:T(8,128)(2,1)S(1)}, bf16[2,4,512,2,96]{2,4,3,1,0:T(8,128)(2,1)S(1)}, u32[]{:S(2)}, u32[]{:S(2)}) collective-permute-start(bf16[2,4,512,2,96]{2,4,3,1,0:T(8,128)(2,1)S(1)} %select_convert_fusion), channel_id=1, source_target_pairs={{0,16},{4,20},{8,24},{12,28},{16,0},{20,4},{24,8},{28,12},{1,17},{... | collective-permute-start | bytes 4718600 | tf_op jit(solution)/shard_map/ppermute | solution.py:21
  952.7 21.4 %copy-start.35 = (pred[1024,512]{0,1:T(8,128)(4,1)S(1)}, pred[1024,512]{0,1:T(8,128)(4,1)}, u32[]{:S(2)}) copy-start(pred[1024,512]{0,1:T(8,128)(4,1)} %copy-done.34) | copy-start | bytes 1572868
  952.7 21.4 %copy-start.49 = (bf16[1024,2,2,96]{0,3,2,1:T(8,128)(2,1)S(1)}, bf16[1024,2,2,96]{0,3,2,1:T(8,128)(2,1)}, u32[]{:S(2)}) copy-start(bf16[1024,2,2,96]{0,3,2,1:T(8,128)(2,1)} %get-tuple-element.726) | copy-start | bytes 2359300
  952.7 20.7 %collective-permute-start.4 = (bf16[2,2,512,2,96]{2,4,3,1,0:T(8,128)(2,1)S(1)}, bf16[2,2,512,2,96]{2,4,3,1,0:T(8,128)(2,1)S(1)}, u32[]{:S(2)}, u32[]{:S(2)}) collective-permute-start(bf16[2,2,512,2,96]{2,4,3,1,0:T(8,128)(2,1)S(1)} %select_convert_fusion.1), channel_id=1, source_target_pairs={{0,8},{4,12},{8,0},{12,4},{16,24},{20,28},{24,16},{28,20},{1,9},{5... | collective-permute-start | bytes 2359304 | tf_op jit(solution)/shard_map/ppermute | solution.py:21
  974.0 2.1 collective-permute-start.5
  980.6 166.1 %reduce-scatter.10.cloned.1.call-start = ((), (), s32[]{:S(2)}) async-start(), calls=%async_computation.10 | async-start | bytes 1769472 | tf_op jit(solution)/shard_map/reduce_scatter | solution.py:272
  989.2 183.6 %all-gather.10.cloned.1.call-start = ((), (), s32[]{:S(2)}) async-start(), calls=%async_computation.13 | async-start | bytes 1327104 | tf_op jit(solution)/shard_map/all_gather | solution.py:293
  990.9 208.4 %all-gather.8.cloned.1.call-start = ((), (), s32[]{:S(2)}) async-start(), calls=%async_computation.9 | async-start | bytes 1327104 | tf_op jit(solution)/shard_map/all_gather | solution.py:284
  992.7 432.9 %all-reduce.12.cloned.1.call-start = ((), (), s32[]{:S(2)}) async-start(), calls=%async_computation.21 | async-start | bytes 12582912 | tf_op jit(solution)/shard_map/psum | solution.py:177
  1161.3 264.2 %copy-start.60 = (f32[1536]{0:T(1024)S(1)}, f32[1536]{0:T(1024)}, u32[]{:S(2)}) copy-start(f32[1536]{0:T(1024)} %param.20) | copy-start | bytes 18436
  1161.3 264.2 %copy-start.63 = (f32[1024]{0:T(1024)S(1)}, f32[1024]{0:T(1024)}, u32[]{:S(2)}) copy-start(f32[1024]{0:T(1024)} %copy-done.62) | copy-start | bytes 12292
  1425.6 42.5 %copy-start.66 = (f32[1024]{0:T(1024)S(1)}, f32[1024]{0:T(1024)}, u32[]{:S(2)}) copy-start(f32[1024]{0:T(1024)} %get-tuple-element.376) | copy-start | bytes 12292
  (105 other events, 402.7 us)
Sparse Core Ops, SparseCore 0:
  286.7 122.2 all-reduce.9
  443.4 217.2 all-gather.17
  664.6 59.9 reduce-scatter.15
  728.8 61.7 reduce-scatter.17
  794.3 61.7 reduce-scatter.19
  860.2 42.4 reduce-scatter.13
  906.7 48.8 reduce-scatter.7
  958.2 35.0 all-gather.11
  995.9 32.3 all-gather.13
  1030.2 32.3 all-gather.15
  1066.2 38.4 reduce-scatter.11
  1108.2 38.4 reduce-scatter.9
  1148.7 24.0 all-gather.9
  1175.3 24.0 all-gather.7
  1202.3 223.1 all-reduce.11
